TPU v7x, 32 devices: a whole 2x2x4 slice. The times are simulated.
32 devices in a mesh: space: 8 (over z, y), band: 4 (over x, core).
Axes of the slice: x: 2, y: 2, z: 4, core: 2. Of those that a mesh axis runs over, the one named last changes fastest.
Arguments:
- columns: float32 [16, 48, 32, 128], P('band', 'space'), may hold values from -6 to 6
- potential: float32 [48, 32, 128], P('space'), may hold values from -1 to 3
- orbitals: float32 [512, 48, 32, 128], P('band', 'space'), may hold values from -0.0546875 to 0.0546875
Outputs:
- projected: float32 [16, 48, 32, 128], P('band', 'space')
- correlation: float32 [512, 16], P('band')
All inputs are finite; a program needn't handle non-finite values.
Results may differ from a plain program's by a relative error of at most 0.00011.
Values sent between devices are 32-bit elements; how exact they have to be, the bound alone decides.
No kernel may reach another device: no remote copies, remote signals or barrier semaphores. Data moves between devices by JAX's collectives and lax.ppermute only.
A program may use at most 128 MiB of HBM per device.

v0:
```python
import jax
import jax.numpy as jnp
from jax import lax
from jax.sharding import PartitionSpec as P

COEFFS = (
    -5369.0 / 1800.0,
    12.0 / 7.0,
    -15.0 / 56.0,
    10.0 / 189.0,
    -1.0 / 112.0,
    2.0 / 1925.0,
    -1.0 / 16632.0,
)


def padded_2(array, sides, width):
    for axis, dim in sides:
        size, length = (lax.axis_size(axis), array.shape[dim])
        up = [(i, (i + 1) % size) for i in range(size)]
        down = [(j, i) for i, j in up]
        last = lax.slice_in_dim(array, length - width, length, axis=dim)
        first = lax.slice_in_dim(array, 0, width, axis=dim)
        before = lax.ppermute(last, axis, up)
        after = lax.ppermute(first, axis, down)
        array = jnp.concatenate([before, array, after], axis=dim)
    return array


def hamiltonian(values, potential):
    padded = padded_2(values, (("space", 1),), 6)
    planes = values.shape[1]
    laplace = 3.0 * COEFFS[0] * values
    for offset in range(1, 7):
        along = (
            padded[:, 6 + offset : 6 + offset + planes]
            + padded[:, 6 - offset : 6 - offset + planes]
        )
        along = along + jnp.roll(values, offset, 2) + jnp.roll(values, -offset, 2)
        along = along + jnp.roll(values, offset, 3) + jnp.roll(values, -offset, 3)
        laplace = laplace + COEFFS[offset] * along
    return -0.5 * laplace + potential[None] * values


def shards(columns, potential, orbitals):
    applied = hamiltonian(columns, potential)
    orb_local = orbitals.shape[0]
    col_local = applied.shape[0]
    psi_flat = orbitals.reshape(orb_local, -1)
    piece = lax.all_gather(applied, "band", axis=0, tiled=True)
    partial_correlation = jnp.einsum(
        "oc,kc->ok", psi_flat, piece.reshape(piece.shape[0], -1), precision=lax.Precision.HIGHEST
    )
    correlation = lax.psum(partial_correlation, "space")
    removed = jnp.einsum("ok,oc->kc", correlation, psi_flat, precision=lax.Precision.HIGHEST)
    removed_all = lax.psum_scatter(
        removed.reshape((col_local * lax.axis_size("band"),) + applied.shape[1:]),
        "band",
        scatter_dimension=0,
        tiled=True,
    )
    projected = applied - removed_all
    return (projected, correlation)


def solution(mesh):
    placed = (
        P("band", "space", None, None),
        P("space", None, None),
        P("band", "space", None, None),
    )
    return jax.shard_map(
        shards,
        mesh=mesh,
        in_specs=placed,
        out_specs=(P("band", "space", None, None), P("band", None)),
        check_vma=False,
    )
```

profile of v0, /device:TPU:0, one launch (start us, length us, event | category | flops | bytes accessed | tf_op | source)
XLA Modules:
  0.0 155.2 jit_solution(5152359355266835999)
XLA Ops:
  7.2 3.0 %collective-permute-start.1 = (f32[4,6,32,128]{3,2,1,0:T(8,128)}, f32[4,6,32,128]{3,2,1,0:T(8,128)S(1)}, u32[]{:S(2)}, u32[]{:S(2)}) collective-permute-start(f32[4,6,32,128]{3,2,1,0:T(8,128)} %param.3), channel_id=1, source_target_pairs={{0,4},{4,8},{8,12},{12,16},{16,20},{20,24},{24,28},{28,0},{1,5},{5... | collective-permute-start | bytes 1179656 | tf_op jit(solution)/shard_map/ppermute | solution.py:24
  10.3 3.1 %collective-permute-start = (f32[4,6,32,128]{3,2,1,0:T(8,128)}, f32[4,6,32,128]{3,2,1,0:T(8,128)S(1)}, u32[]{:S(2)}, u32[]{:S(2)}) collective-permute-start(f32[4,6,32,128]{3,2,1,0:T(8,128)} %param.3), channel_id=1, source_target_pairs={{4,0},{8,4},{12,8},{16,12},{20,16},{24,20},{28,24},{0,28},{5,1},{9... | collective-permute-start | bytes 1179656 | tf_op jit(solution)/shard_map/ppermute | solution.py:25
  13.4 1.3 fusion.69
  14.6 1.4 fusion.67
  16.0 1.4 fusion.68
  17.4 1.3 fusion.65
  18.6 1.4 fusion.63
  20.0 1.4 fusion.64
  21.4 1.3 fusion.61
  22.6 1.0 fusion.62
  23.6 1.4 fusion.59
  25.0 0.2 fusion.60
  25.2 0.1 fusion.57
  25.3 0.2 fusion.55
  25.4 0.2 fusion.56
  25.7 0.2 fusion.51
  25.9 0.2 fusion.52
  26.2 0.2 fusion.47
  26.4 0.2 fusion.48
  26.6 0.8 collective-permute-done.1
  27.4 0.1 constant_dynamic-update-slice_fusion.1
  27.5 2.0 %collective-permute-done = f32[4,6,32,128]{3,2,1,0:T(8,128)S(1)} collective-permute-done((f32[4,6,32,128]{3,2,1,0:T(8,128)}, f32[4,6,32,128]{3,2,1,0:T(8,128)S(1)}, u32[]{:S(2)}, u32[]{:S(2)}) %collective-permute-start) | collective-permute-done | bytes 393248 | tf_op jit(solution)/shard_map/ppermute | solution.py:25
  29.5 3.8 %fusion.16 = f32[4,6,32,128]{3,2,1,0:T(8,128)} fusion(f32[4,12,32,128]{3,2,1,0:T(8,128)S(1)} %get-tuple-element.53, f32[4,12,32,128]{3,2,1,0:T(8,128)S(1)} %constant_dynamic-update-slice_fusion, f32[4,6,31,128]{3,2,1,0:T(8,128)S(1)} %get-tuple-element.49, f32[4,6,1,128]{3,2,1,0:T(1,128)S(1)} %get-tuple-element.51, ...), kind=kLoop, calls=%fused_computation.14 | loop fusion | flops 6881280 | bytes 15040512 | tf_op jit(solution)/shard_map/add | solution.py:42
  33.3 0.2 reduce-scatter.2.cloned.1.call-start
  33.6 18.9 %copy.78 = f32[16,8,192,128]{3,1,2,0:T(8,128)} copy(f32[16,8,192,128]{3,2,1,0:T(8,128)} %bitcast.21) | data formatting | bytes 25165824
  52.5 12.6 %copy.64 = f32[24576,128]{1,0:T(8,128)} copy(f32[24576,128]{0,1:T(8,128)} %bitcast.23) | data formatting | bytes 25165824 | tf_op jit(solution)/shard_map/ok,oc->kc/dot_general | solution.py:55
  65.1 20.7 %fusion.3 = f32[128,16]{0,1:T(8,128)S(1)} fusion(f32[128,6,32,128]{3,2,1,0:T(8,128)} %param.5, f32[16,6,32,128]{3,2,1,0:T(8,128)} %all-gather.2.cloned.1.call-done), kind=kOutput, calls=%fused_computation.4 | convolution fusion | flops 603979776 | bytes 14163968 | tf_op jit(solution)/shard_map/oc,kc->ok/dot_general | solution.py:51
  85.8 21.0 %psum.7 = f32[128,16]{0,1:T(8,128)S(1)} all-reduce(f32[128,16]{0,1:T(8,128)S(1)} %fusion.3), channel_id=1, replica_groups=mesh['space'=8,'band'=4] {'space'}, use_global_device_ids=true, to_apply=%region_0.1 | all-reduce | flops 2048 | bytes 16384 | tf_op jit(solution)/shard_map/psum | solution.py:54
  106.7 12.7 %fusion.45 = f32[16,6,32,128]{3,0,2,1:T(8,128)S(1)} fusion(f32[6,32,128,128]{3,2,1,0:T(8,128)} %bitcast.22, f32[128,16]{0,1:T(8,128)S(1)} %psum.7), kind=kOutput, calls=%fused_computation.52 | convolution fusion | flops 603979776 | bytes 14163968 | tf_op jit(solution)/shard_map/ok,oc->kc/dot_general | solution.py:55
  119.5 1.7 %copy.65 = f32[16,6,32,128]{3,2,1,0:T(8,128)} copy(f32[16,6,32,128]{3,0,2,1:T(8,128)S(1)} %fusion.45) | data formatting | bytes 3145728 | tf_op jit(solution)/shard_map/ok,oc->kc/dot_general | solution.py:55
  121.2 25.4 %reduce-scatter.2.cloned.1.call-done = f32[4,6,32,128]{3,2,1,0:T(8,128)} async-done(((f32[16,6,32,128]{3,2,1,0:T(8,128)}), f32[4,6,32,128]{3,2,1,0:T(8,128)}) %reduce-scatter.2.cloned.1.call-update) | async-done | bytes 393232 | tf_op jit(solution)/shard_map/reduce_scatter | solution.py:56
  146.6 1.8 %sub.3 = f32[4,6,32,128]{3,2,1,0:T(8,128)} subtract(f32[4,6,32,128]{3,2,1,0:T(8,128)S(1)} %copy-done.1, f32[4,6,32,128]{3,2,1,0:T(8,128)} %reduce-scatter.2.cloned.1.call-done) | non-fusion elementwise | flops 98304 | bytes 1179648 | tf_op jit(solution)/shard_map/sub | solution.py:62
  (21 shorter events, 0.4 us)
Async XLA Ops:
  7.2 17.8 %copy-start = (f32[4,6,32,128]{3,2,1,0:T(8,128)S(1)}, f32[4,6,32,128]{3,2,1,0:T(8,128)}, u32[]{:S(2)}) copy-start(f32[4,6,32,128]{3,2,1,0:T(8,128)} %param.3) | copy-start | bytes 1179652
  7.2 57.9 %all-gather.2.cloned.1.call-start = ((), (), s32[]{:S(2)}) async-start(), calls=%async_computation.1 | async-start | bytes 1966080 | tf_op jit(solution)/shard_map/all_gather | solution.py:50
  7.2 20.2 %collective-permute-start.1 = (f32[4,6,32,128]{3,2,1,0:T(8,128)}, f32[4,6,32,128]{3,2,1,0:T(8,128)S(1)}, u32[]{:S(2)}, u32[]{:S(2)}) collective-permute-start(f32[4,6,32,128]{3,2,1,0:T(8,128)} %param.3), channel_id=1, source_target_pairs={{0,4},{4,8},{8,12},{12,16},{16,20},{20,24},{24,28},{28,0},{1,5},{5... | collective-permute-start | bytes 1179656 | tf_op jit(solution)/shard_map/ppermute | solution.py:24
  10.3 19.2 %collective-permute-start = (f32[4,6,32,128]{3,2,1,0:T(8,128)}, f32[4,6,32,128]{3,2,1,0:T(8,128)S(1)}, u32[]{:S(2)}, u32[]{:S(2)}) collective-permute-start(f32[4,6,32,128]{3,2,1,0:T(8,128)} %param.3), channel_id=1, source_target_pairs={{4,0},{8,4},{12,8},{16,12},{20,16},{24,20},{28,24},{0,28},{5,1},{9... | collective-permute-start | bytes 1179656 | tf_op jit(solution)/shard_map/ppermute | solution.py:25
  20.0 9.5 %copy-start.2 = (f32[6,32,128]{2,1,0:T(8,128)S(1)}, f32[6,32,128]{2,1,0:T(8,128)}, u32[]{:S(2)}) copy-start(f32[6,32,128]{2,1,0:T(8,128)} %param.4) | copy-start | bytes 294916
  33.3 113.2 %reduce-scatter.2.cloned.1.call-start = ((), (), s32[]{:S(2)}) async-start(), calls=%async_computation.2 | async-start | bytes 1966080 | tf_op jit(solution)/shard_map/reduce_scatter | solution.py:56
  85.7 60.8 %copy-start.1 = (f32[4,6,32,128]{3,2,1,0:T(8,128)S(1)}, f32[4,6,32,128]{3,2,1,0:T(8,128)}, u32[]{:S(2)}) copy-start(f32[4,6,32,128]{3,2,1,0:T(8,128)} %fusion.16) | copy-start | bytes 1179652
  106.7 41.6 %copy-start.3 = (f32[128,16]{0,1:T(8,128)}, f32[128,16]{0,1:T(8,128)S(1)}, u32[]{:S(2)}) copy-start(f32[128,16]{0,1:T(8,128)S(1)} %psum.7) | copy-start | bytes 24580
Sparse Core Ops, SparseCore 0:
  33.5 19.7 all-gather.1
  121.3 25.2 reduce-scatter.1
where the time goes:
time: 156 us; the launch traced here: 155 us
  local copies, waits for them, and re-layouts  46.5 us (30%)
  matrix products  33.4 us (21%)
  waiting for transfers between devices  28.2 us (18%)
  blocking collectives  21 us (13%)
  between operations  14.2 us (9%)
  starting transfers between devices  6.41 us (4%)
  other arithmetic  5.59 us (4%)
    reduce_scatter x1, waiting for transfers between devices, shards(): lax.psum_scatter(removed.reshape((col_local * lax.axis_size('band'),) + a...  25.4 us
    psum x1, blocking collectives, shards(): correlation = lax.psum(partial_correlation, 'space')  21 us
    dot_general x1, matrix products, shards(): jnp.einsum('oc,kc->ok', psi_flat, piece.reshape(piece.shape[0], -1), prec...  20.7 us
    unnamed x11, local copies, waits for them, and re-layouts  19 us
    dot_general x2, local copies, waits for them, and re-layouts, shards(): jnp.einsum('ok,oc->kc', correlation, psi_flat, precision=lax.Precision.HI...  14.3 us
    dot_general x1, matrix products, shards(): jnp.einsum('ok,oc->kc', correlation, psi_flat, precision=lax.Precision.HI...  12.7 us
    slice x12, local copies, waits for them, and re-layouts, hamiltonian(): along = along + jnp.roll(values, offset, 3) + jnp.roll(values, -offset, 3)  8.09 us
    slice x12, local copies, waits for them, and re-layouts, hamiltonian(): along = along + jnp.roll(values, offset, 2) + jnp.roll(values, -offset, 2)  5.05 us
  transfers between devices with their start and end apart: 4, of which 3 were waited for; matrix products, arithmetic and copies ran while one was open for 29% of the time, Pallas kernels for 0%

commit v1 on v0

--- a/solution.py
+++ b/solution.py
@@ -51,7 +51,17 @@
     partial_correlation = jnp.einsum(
         "oc,kc->ok", psi_flat, piece.reshape(piece.shape[0], -1), precision=lax.Precision.HIGHEST
     )
-    correlation = lax.psum(partial_correlation, "space")
+    correlation, z2 = (partial_correlation, 0)
+    n_shards = lax.axis_size("space")
+    while 1 << z2 < n_shards:
+        history = []
+        jj = 0
+        while jj < n_shards:
+            history.append((jj, jj ^ 1 << z2))
+            jj += 1
+        outcome_arr = lax.ppermute(correlation, "space", perm=history)
+        correlation = correlation + outcome_arr
+        z2 = z2 + 1
     removed = jnp.einsum("ok,oc->kc", correlation, psi_flat, precision=lax.Precision.HIGHEST)
     removed_all = lax.psum_scatter(
         removed.reshape((col_local * lax.axis_size("band"),) + applied.shape[1:]),

time: 156 us -> 166 us (1.064)
  waiting for transfers between devices: 28.2 us -> 53.3 us
  blocking collectives: 21 us -> 0 us
  starting transfers between devices: 6.41 us -> 11.7 us
    psum x1 -> x0, blocking collectives: 21 us -> none  [shards(): correlation = lax.psum(partial_correlation, 'space')]
    all_gather x1, waiting for transfers between devices: 0.01 us -> 19.9 us  [shards(): piece = lax.all_gather(applied, 'band', axis=0, tiled=True)]
    ppermute x0 -> x3, starting transfers between devices: none -> 5.43 us  [shards(): outcome_arr = lax.ppermute(correlation, 'space', perm=history)]
    ppermute x0 -> x3, waiting for transfers between devices: none -> 4.35 us  [shards(): outcome_arr = lax.ppermute(correlation, 'space', perm=history)]
  transfers between devices with their start and end apart: 4 -> 7, of which waited for: 3 -> 6; matrix products, arithmetic and copies ran while one was open for 29% -> 27% of each run, Pallas kernels for 0% -> 0%
where the time goes in v1:
time: 166 us; the launch traced here: 165 us
  waiting for transfers between devices  53.3 us (32%)
  local copies, waits for them, and re-layouts  46.5 us (28%)
  matrix products  33.7 us (20%)
  between operations  14.2 us (9%)
  starting transfers between devices  11.7 us (7%)
  other arithmetic  5.6 us (3%)
    reduce_scatter x1, waiting for transfers between devices, shards(): lax.psum_scatter(removed.reshape((col_local * lax.axis_size('band'),) + a...  26.4 us
    dot_general x1, matrix products, shards(): jnp.einsum('oc,kc->ok', psi_flat, piece.reshape(piece.shape[0], -1), prec...  20.8 us
    all_gather x1, waiting for transfers between devices, shards(): piece = lax.all_gather(applied, 'band', axis=0, tiled=True)  19.9 us
    unnamed x11, local copies, waits for them, and re-layouts  19 us
    dot_general x2, local copies, waits for them, and re-layouts, shards(): jnp.einsum('ok,oc->kc', correlation, psi_flat, precision=lax.Precision.HI...  14.3 us
    dot_general x1, matrix products, shards(): jnp.einsum('ok,oc->kc', correlation, psi_flat, precision=lax.Precision.HI...  12.9 us
    slice x12, local copies, waits for them, and re-layouts, hamiltonian(): along = along + jnp.roll(values, offset, 3) + jnp.roll(values, -offset, 3)  8.09 us
    ppermute x3, starting transfers between devices, shards(): outcome_arr = lax.ppermute(correlation, 'space', perm=history)  5.43 us
  transfers between devices with their start and end apart: 7, of which 6 were waited for; matrix products, arithmetic and copies ran while one was open for 27% of the time, Pallas kernels for 0%

profile of v1, /device:TPU:0, one launch (start us, length us, event | category | flops | bytes accessed | tf_op | source)
XLA Modules:
  0.0 165.0 jit_solution(17690337462435963354)
XLA Ops:
  7.2 3.0 %collective-permute-start.1 = (f32[4,6,32,128]{3,2,1,0:T(8,128)}, f32[4,6,32,128]{3,2,1,0:T(8,128)S(1)}, u32[]{:S(2)}, u32[]{:S(2)}) collective-permute-start(f32[4,6,32,128]{3,2,1,0:T(8,128)} %param.3), channel_id=1, source_target_pairs={{0,4},{4,8},{8,12},{12,16},{16,20},{20,24},{24,28},{28,0},{1,5},{5... | collective-permute-start | bytes 1179656 | tf_op jit(solution)/shard_map/ppermute | solution.py:24
  10.3 3.1 %collective-permute-start = (f32[4,6,32,128]{3,2,1,0:T(8,128)}, f32[4,6,32,128]{3,2,1,0:T(8,128)S(1)}, u32[]{:S(2)}, u32[]{:S(2)}) collective-permute-start(f32[4,6,32,128]{3,2,1,0:T(8,128)} %param.3), channel_id=1, source_target_pairs={{4,0},{8,4},{12,8},{16,12},{20,16},{24,20},{28,24},{0,28},{5,1},{9... | collective-permute-start | bytes 1179656 | tf_op jit(solution)/shard_map/ppermute | solution.py:25
  13.4 1.3 fusion.69
  14.6 1.4 fusion.67
  16.0 1.4 fusion.68
  17.4 1.3 fusion.65
  18.6 1.4 fusion.63
  20.0 1.4 fusion.64
  21.4 1.3 fusion.61
  22.6 1.0 fusion.62
  23.6 1.4 fusion.59
  25.3 0.2 fusion.55
  25.4 0.2 fusion.56
  25.7 0.2 fusion.51
  25.9 0.2 fusion.52
  26.4 0.2 fusion.48
  26.6 0.8 collective-permute-done.1
  27.5 2.0 %collective-permute-done = f32[4,6,32,128]{3,2,1,0:T(8,128)S(1)} collective-permute-done((f32[4,6,32,128]{3,2,1,0:T(8,128)}, f32[4,6,32,128]{3,2,1,0:T(8,128)S(1)}, u32[]{:S(2)}, u32[]{:S(2)}) %collective-permute-start) | collective-permute-done | bytes 393248 | tf_op jit(solution)/shard_map/ppermute | solution.py:25
  29.5 3.8 %fusion.16 = f32[4,6,32,128]{3,2,1,0:T(8,128)} fusion(f32[4,12,32,128]{3,2,1,0:T(8,128)S(1)} %get-tuple-element.53, f32[4,12,32,128]{3,2,1,0:T(8,128)S(1)} %constant_dynamic-update-slice_fusion, f32[4,6,31,128]{3,2,1,0:T(8,128)S(1)} %get-tuple-element.49, f32[4,6,1,128]{3,2,1,0:T(1,128)S(1)} %get-tuple-element.51, ...), kind=kLoop, calls=%fused_computation.14 | loop fusion | flops 6881280 | bytes 15040512 | tf_op jit(solution)/shard_map/add | solution.py:42
  33.4 19.9 %all-gather.2.cloned.1.call-done = f32[16,6,32,128]{3,2,1,0:T(8,128)} async-done(((f32[4,6,32,128]{3,2,1,0:T(8,128)}), f32[16,6,32,128]{3,2,1,0:T(8,128)}) %all-gather.2.cloned.1.call-update) | async-done | bytes 1572880 | tf_op jit(solution)/shard_map/all_gather | solution.py:50
  53.3 20.8 %fusion.3 = f32[128,16]{0,1:T(8,128)S(1)} fusion(f32[128,6,32,128]{3,2,1,0:T(8,128)} %param.5, f32[16,6,32,128]{3,2,1,0:T(8,128)} %all-gather.2.cloned.1.call-done), kind=kOutput, calls=%fused_computation.4 | convolution fusion | flops 603979776 | bytes 14163968 | tf_op jit(solution)/shard_map/oc,kc->ok/dot_general | solution.py:51
  74.0 1.5 collective-permute-start.2
  75.6 2.2 %collective-permute-done.2 = f32[128,16]{0,1:T(8,128)S(1)} collective-permute-done((f32[128,16]{0,1:T(8,128)S(1)}, f32[128,16]{0,1:T(8,128)S(1)}, u32[]{:S(2)}, u32[]{:S(2)}) %collective-permute-start.2) | collective-permute-done | bytes 8224 | tf_op jit(solution)/shard_map/ppermute | solution.py:62
  77.8 1.5 collective-permute-start.3
  79.2 2.2 %collective-permute-done.3 = f32[128,16]{0,1:T(8,128)S(1)} collective-permute-done((f32[128,16]{0,1:T(8,128)S(1)}, f32[128,16]{0,1:T(8,128)S(1)}, u32[]{:S(2)}, u32[]{:S(2)}) %collective-permute-start.3) | collective-permute-done | bytes 8224 | tf_op jit(solution)/shard_map/ppermute | solution.py:62
  81.4 2.4 %collective-permute-start.4 = (f32[128,16]{0,1:T(8,128)S(1)}, f32[128,16]{0,1:T(8,128)S(1)}, u32[]{:S(2)}, u32[]{:S(2)}) collective-permute-start(f32[128,16]{0,1:T(8,128)S(1)} %add.160), channel_id=1, source_target_pairs={{0,16},{4,20},{8,24},{12,28},{16,0},{20,4},{24,8},{28,12},{1,17},{... | collective-permute-start | bytes 24584 | tf_op jit(solution)/shard_map/ppermute | solution.py:62
  83.8 18.9 %copy.78 = f32[16,8,192,128]{3,1,2,0:T(8,128)} copy(f32[16,8,192,128]{3,2,1,0:T(8,128)} %bitcast.21) | data formatting | bytes 25165824
  102.7 12.6 %copy.64 = f32[24576,128]{1,0:T(8,128)} copy(f32[24576,128]{0,1:T(8,128)} %bitcast.23) | data formatting | bytes 25165824 | tf_op jit(solution)/shard_map/ok,oc->kc/dot_general | solution.py:65
  115.4 12.9 %fusion.45 = f32[16,6,32,128]{3,0,2,1:T(8,128)S(1)} fusion(f32[6,32,128,128]{3,2,1,0:T(8,128)} %bitcast.22, f32[128,16]{0,1:T(8,128)S(1)} %add.161), kind=kOutput, calls=%fused_computation.52 | convolution fusion | flops 603979776 | bytes 14163968 | tf_op jit(solution)/shard_map/ok,oc->kc/dot_general | solution.py:65
  128.3 1.7 %copy.65 = f32[16,6,32,128]{3,2,1,0:T(8,128)} copy(f32[16,6,32,128]{3,0,2,1:T(8,128)S(1)} %fusion.45) | data formatting | bytes 3145728 | tf_op jit(solution)/shard_map/ok,oc->kc/dot_general | solution.py:65
  130.0 26.4 %reduce-scatter.2.cloned.1.call-done = f32[4,6,32,128]{3,2,1,0:T(8,128)} async-done(((f32[16,6,32,128]{3,2,1,0:T(8,128)}), f32[4,6,32,128]{3,2,1,0:T(8,128)}) %reduce-scatter.2.cloned.1.call-update) | async-done | bytes 393232 | tf_op jit(solution)/shard_map/reduce_scatter | solution.py:66
  156.4 1.8 %sub.3 = f32[4,6,32,128]{3,2,1,0:T(8,128)} subtract(f32[4,6,32,128]{3,2,1,0:T(8,128)S(1)} %copy-done.1, f32[4,6,32,128]{3,2,1,0:T(8,128)} %reduce-scatter.2.cloned.1.call-done) | non-fusion elementwise | flops 98304 | bytes 1179648 | tf_op jit(solution)/shard_map/sub | solution.py:72
  (29 shorter events, 0.9 us)
Async XLA Ops:
  7.2 17.8 %copy-start = (f32[4,6,32,128]{3,2,1,0:T(8,128)S(1)}, f32[4,6,32,128]{3,2,1,0:T(8,128)}, u32[]{:S(2)}) copy-start(f32[4,6,32,128]{3,2,1,0:T(8,128)} %param.3) | copy-start | bytes 1179652
  7.2 46.1 %all-gather.2.cloned.1.call-start = ((), (), s32[]{:S(2)}) async-start(), calls=%async_computation.1 | async-start | bytes 1966080 | tf_op jit(solution)/shard_map/all_gather | solution.py:50
  7.2 20.2 %collective-permute-start.1 = (f32[4,6,32,128]{3,2,1,0:T(8,128)}, f32[4,6,32,128]{3,2,1,0:T(8,128)S(1)}, u32[]{:S(2)}, u32[]{:S(2)}) collective-permute-start(f32[4,6,32,128]{3,2,1,0:T(8,128)} %param.3), channel_id=1, source_target_pairs={{0,4},{4,8},{8,12},{12,16},{16,20},{20,24},{24,28},{28,0},{1,5},{5... | collective-permute-start | bytes 1179656 | tf_op jit(solution)/shard_map/ppermute | solution.py:24
  10.3 19.2 %collective-permute-start = (f32[4,6,32,128]{3,2,1,0:T(8,128)}, f32[4,6,32,128]{3,2,1,0:T(8,128)S(1)}, u32[]{:S(2)}, u32[]{:S(2)}) collective-permute-start(f32[4,6,32,128]{3,2,1,0:T(8,128)} %param.3), channel_id=1, source_target_pairs={{4,0},{8,4},{12,8},{16,12},{20,16},{24,20},{28,24},{0,28},{5,1},{9... | collective-permute-start | bytes 1179656 | tf_op jit(solution)/shard_map/ppermute | solution.py:25
  20.0 9.5 %copy-start.2 = (f32[6,32,128]{2,1,0:T(8,128)S(1)}, f32[6,32,128]{2,1,0:T(8,128)}, u32[]{:S(2)}) copy-start(f32[6,32,128]{2,1,0:T(8,128)} %param.4) | copy-start | bytes 294916
  33.3 123.0 %reduce-scatter.2.cloned.1.call-start = ((), (), s32[]{:S(2)}) async-start(), calls=%async_computation.2 | async-start | bytes 1966080 | tf_op jit(solution)/shard_map/reduce_scatter | solution.py:66
  74.0 3.7 %collective-permute-start.2 = (f32[128,16]{0,1:T(8,128)S(1)}, f32[128,16]{0,1:T(8,128)S(1)}, u32[]{:S(2)}, u32[]{:S(2)}) collective-permute-start(f32[128,16]{0,1:T(8,128)S(1)} %fusion.3), channel_id=1, source_target_pairs={{0,4},{4,0},{8,12},{12,8},{16,20},{20,16},{24,28},{28,24},{1,5},{5... | collective-permute-start | bytes 24584 | tf_op jit(solution)/shard_map/ppermute | solution.py:62
  77.8 3.7 %collective-permute-start.3 = (f32[128,16]{0,1:T(8,128)S(1)}, f32[128,16]{0,1:T(8,128)S(1)}, u32[]{:S(2)}, u32[]{:S(2)}) collective-permute-start(f32[128,16]{0,1:T(8,128)S(1)} %add.159), channel_id=1, source_target_pairs={{0,8},{4,12},{8,0},{12,4},{16,24},{20,28},{24,16},{28,20},{1,9},{5... | collective-permute-start | bytes 24584 | tf_op jit(solution)/shard_map/ppermute | solution.py:62
  81.4 33.9 %collective-permute-start.4 = (f32[128,16]{0,1:T(8,128)S(1)}, f32[128,16]{0,1:T(8,128)S(1)}, u32[]{:S(2)}, u32[]{:S(2)}) collective-permute-start(f32[128,16]{0,1:T(8,128)S(1)} %add.160), channel_id=1, source_target_pairs={{0,16},{4,20},{8,24},{12,28},{16,0},{20,4},{24,8},{28,12},{1,17},{... | collective-permute-start | bytes 24584 | tf_op jit(solution)/shard_map/ppermute | solution.py:62
  115.4 41.0 %copy-start.1 = (f32[4,6,32,128]{3,2,1,0:T(8,128)S(1)}, f32[4,6,32,128]{3,2,1,0:T(8,128)}, u32[]{:S(2)}) copy-start(f32[4,6,32,128]{3,2,1,0:T(8,128)} %fusion.16) | copy-start | bytes 1179652
  115.4 42.8 %copy-start.3 = (f32[128,16]{0,1:T(8,128)}, f32[128,16]{0,1:T(8,128)S(1)}, u32[]{:S(2)}) copy-start(f32[128,16]{0,1:T(8,128)S(1)} %add.161) | copy-start | bytes 24580
Sparse Core Ops, SparseCore 0:
  33.5 19.7 all-gather.1
  130.1 26.1 reduce-scatter.1
